TPU v7x, 256 devices: a whole 4x4x8 slice. The times are simulated.
256 devices in a mesh: tm: 64 (over z, y, core), site: 4 (over x).
Axes of the slice: x: 4, y: 4, z: 8, core: 2. Of those that a mesh axis runs over, the one named last changes fastest.
Arguments:
- obs_rows: bfloat16 [131072, 256], P(('tm', 'site')), may hold values from -2 to 2
- obs_values: bfloat16 [131072], P(('tm', 'site')), may hold values from -6 to 6
- obs_hours: int32 [131072], P(('tm', 'site')), may hold values from 0 to 3
- prior_precision: float32 [256, 256], replicated, may hold values from -1 to 3, as said below
- transition: float32 [256, 256], replicated, may hold values from -1 to 1
- site_basis: bfloat16 [1048576, 256], P(('tm', 'site')), may hold values from -0.375 to 0.375
Outputs:
- prediction: bfloat16 [256, 1048576], P(None, ('tm', 'site'))
Inputs may be any that keep to these rules, and one draw needn't show every extreme that they name: `prior_precision`: symmetric and positive definite.
All inputs are finite; a program needn't handle non-finite values. Where the computation divides by a largest or mean magnitude, that divisor is 1e-20 or more.
Results may differ from a plain program's by a relative error of at most 0.0049.
Values may be sent and summed in bfloat16 or wider, within the bound.
A program may use at most 64 MiB of HBM per device.

v0:
```python
import jax
import jax.numpy as jnp
from jax import lax
from jax.sharding import PartitionSpec as P

NS_ITERS = 8


def entering(part, axis, combine, identity):
    place = lax.axis_index(axis)
    gathered = jax.tree.map(lambda a: lax.all_gather(a, axis), part)
    state = jax.tree.map(lambda a, e: jnp.zeros_like(a) + jnp.asarray(e, a.dtype), part, identity)

    def one(turn, state):
        return combine(
            state, jax.tree.map(lambda a: lax.dynamic_index_in_dim(a, turn, 0, False), gathered)
        )

    return lax.fori_loop(0, place, one, state)


def approx_inverse(precisions):
    states = precisions.shape[-1]
    bounds = jnp.max(jnp.sum(jnp.abs(precisions), axis=2), axis=1)
    identity = jnp.eye(states, dtype=jnp.float32)
    inverse = identity[None] / bounds[:, None, None]
    for iteration in range(NS_ITERS):
        product = jnp.einsum("hij,hjk->hik", precisions, inverse, precision=lax.Precision.HIGHEST)
        inverse = jnp.einsum(
            "hij,hjk->hik", inverse, 2.0 * identity - product, precision=lax.Precision.HIGHEST
        )
    return inverse


def compose(earlier, latter):
    joined_map = jnp.dot(latter[0], earlier[0], precision=lax.Precision.HIGHEST)
    joined_shift = jnp.dot(latter[0], earlier[1], precision=lax.Precision.HIGHEST) + latter[1]
    return (joined_map, joined_shift)


def hour_elements(summed_grams, drives, prior_precision, coupled):
    inverse = approx_inverse(prior_precision[None] + summed_grams)
    hour_maps = jnp.einsum("hij,jk->hik", inverse, coupled, precision=lax.Precision.HIGHEST)
    offsets = jnp.einsum("hij,hj->hi", inverse, drives, precision=lax.Precision.HIGHEST)
    return (hour_maps, offsets)


def body(obs_rows, obs_values, obs_hours, prior_precision, transition, site_basis):
    blocks = lax.axis_size("site")
    row_count = obs_rows.shape[0]
    hour_slot = lax.broadcasted_iota(jnp.int32, (blocks, row_count), 0)
    member = obs_hours[None, :] == hour_slot
    masked = jnp.where(member[:, :, None], obs_rows[None], jnp.zeros((), jnp.bfloat16))
    local_grams = jnp.einsum("hrs,rt->hst", masked, obs_rows, preferred_element_type=jnp.float32)
    weighted = jnp.where(member, obs_values[None], jnp.zeros((), jnp.bfloat16))
    local_drives = jnp.einsum("hr,rs->hs", weighted, obs_rows, preferred_element_type=jnp.float32)
    summed_grams, drives = (
        lax.psum_scatter(local_grams, "site", scatter_dimension=0, tiled=True),
        lax.psum_scatter(local_drives, "site", scatter_dimension=0, tiled=True),
    )
    coupled = jnp.dot(prior_precision, transition, precision=lax.Precision.HIGHEST)
    states = transition.shape[0]
    identity = jnp.eye(states, dtype=jnp.float32)
    zero_state = jnp.zeros((states,), jnp.float32)
    hour_maps, offsets = hour_elements(summed_grams, drives, prior_precision, coupled)
    block_maps, block_offsets = (
        lax.all_gather(hour_maps, "site", axis=0, tiled=True),
        lax.all_gather(offsets, "site", axis=0, tiled=True),
    )
    joined = (block_maps[0], block_offsets[0])
    for position in range(1, blocks):
        joined = compose(joined, (block_maps[position], block_offsets[position]))
    before = entering(joined, "tm", compose, (identity, zero_state))
    state_mean = before[1]
    results = []
    for position in range(blocks):
        state_mean = (
            jnp.dot(block_maps[position], state_mean, precision=lax.Precision.HIGHEST)
            + block_offsets[position]
        )
        results.append(state_mean)
    rounded = jnp.stack(results).astype(jnp.bfloat16)
    return jnp.einsum(
        "hs,ns->hn",
        lax.all_gather(rounded, "tm", axis=0, tiled=True),
        site_basis,
        preferred_element_type=jnp.float32,
    ).astype(jnp.bfloat16)


def solution(mesh):
    in_specs = (
        P(("tm", "site"), None),
        P(("tm", "site")),
        P(("tm", "site")),
        P(),
        P(),
        P(("tm", "site"), None),
    )
    out_specs = P(None, ("tm", "site"))
    return jax.shard_map(body, mesh=mesh, in_specs=in_specs, out_specs=out_specs, check_vma=False)
```

profile of v0, /device:TPU:1, one launch (start us, length us, event | category | flops | bytes accessed | tf_op | source)
XLA Modules:
  0.0 322.2 jit_solution(5100696245763074373)
XLA Ops:
  6.5 1.2 copy.8
  7.8 0.7 iota_compare_fusion.3
  8.5 2.4 fusion.4
  10.9 0.4 fusion.68
  11.3 28.3 %reduce-scatter.2.cloned.1.call-done = f32[1,256,256]{2,1,0:T(8,128)} async-done(((f32[4,256,256]{2,1,0:T(8,128)}), f32[1,256,256]{2,1,0:T(8,128)}) %reduce-scatter.2.cloned.1.call-update) | async-done | bytes 262160 | tf_op jit(solution)/shard_map/reduce_scatter | solution.py:58
  39.6 1.1 abs_reduce_fusion
  40.7 0.6 reduce_max.9
  42.0 0.4 convolution_subtract_fusion.7
  42.7 0.4 convolution_subtract_fusion.6
  43.5 0.4 convolution_subtract_fusion.5
  44.3 0.4 convolution_subtract_fusion.4
  45.1 0.4 convolution_subtract_fusion.3
  45.8 0.4 convolution_subtract_fusion.2
  46.6 0.4 convolution_subtract_fusion.1
  47.4 0.4 convolution_subtract_fusion
  47.8 0.4 fusion.67
  48.2 1.1 fusion.69
  49.4 26.0 %all-gather.10.cloned.1.call-done = f32[1024,256]{1,0:T(8,128)} async-done(((f32[256,256]{1,0:T(8,128)}), f32[1024,256]{1,0:T(8,128)}) %all-gather.10.cloned.1.call-update) | async-done | bytes 1048592 | tf_op jit(solution)/shard_map/all_gather | solution.py:67
  75.3 1.5 fusion.21
  76.8 1.3 fusion.32
  78.2 2.0 fusion.38
  80.2 0.6 dynamic-slice
  80.8 1.1 fusion.46
  81.9 7.7 %all-reduce = f32[4,256]{1,0:T(4,128)S(1)} all-reduce(f32[4,256]{1,0:T(4,128)S(1)} %fusion.46), channel_id=7, replica_groups=mesh['tm'=64,'site'=4] {'site'}, use_global_device_ids=true, to_apply=%region_3.4.clone | all-reduce | flops 1024 | bytes 8192
  89.6 0.9 convolution_bitcast_fusion
  90.5 5.3 %all-gather.4 = f32[4,1,256]{2,1,0:T(1,128)S(1)} all-gather(f32[1,1,256]{2,1,0:T(1,128)S(1)} %convolution_bitcast_fusion), channel_id=4, replica_groups=mesh['tm'=64,'site'=4] {'site'}, dimensions={0}, use_global_device_ids=true | all-gather | bytes 5120 | tf_op jit(solution)/shard_map/all_gather | solution.py:68
  96.8 51.4 %all-gather.5 = f32[64,1,256]{2,1,0:T(1,128)S(1)} all-gather(f32[1,1,256]{2,1,0:T(1,128)S(1)} %bitcast.138), channel_id=5, replica_groups=mesh['tm'=64,'site'=4] {'tm'}, dimensions={0}, use_global_device_ids=true | all-gather | bytes 66560 | tf_op jit(solution)/shard_map/all_gather | solution.py:11
  148.1 34.4 %all-gather.12.cloned.1.call-done = f32[16384,256]{1,0:T(8,128)} async-done(((f32[256,256]{1,0:T(8,128)}), f32[16384,256]{1,0:T(8,128)}) %all-gather.12.cloned.1.call-update) | async-done | bytes 16777232 | tf_op jit(solution)/shard_map/all_gather | solution.py:11
  182.5 1.3 while.12
  182.5 1.2 fusion.114
  185.2 128.3 %all-gather.6 = bf16[64,4,256]{2,1,0:T(4,128)(2,1)S(1)} all-gather(bf16[1,4,256]{2,1,0:T(4,128)(2,1)S(1)} %maximum_bitcast_fusion), channel_id=1, replica_groups=mesh['tm'=64,'site'=4] {'tm'}, dimensions={0}, use_global_device_ids=true | all-gather | bytes 133120 | tf_op jit(solution)/shard_map/all_gather | solution.py:85
  313.6 2.1 convolution_convert_fusion
  (52 shorter events, 5.0 us)
Async XLA Ops:
  6.5 307.1 %copy-start = (bf16[4096,256]{1,0:T(8,128)(2,1)S(1)}, bf16[4096,256]{1,0:T(8,128)(2,1)}, u32[]{:S(2)}) copy-start(bf16[4096,256]{1,0:T(8,128)(2,1)} %param.13) | copy-start | bytes 6291460
  6.5 4.4 %copy-start.2 = (f32[256,256]{1,0:T(8,128)S(1)}, f32[256,256]{1,0:T(8,128)}, u32[]{:S(2)}) copy-start(f32[256,256]{1,0:T(8,128)} %param.11) | copy-start | bytes 786436
  6.5 4.4 %copy-start.3 = (f32[256,256]{1,0:T(8,128)S(1)}, f32[256,256]{1,0:T(8,128)}, u32[]{:S(2)}) copy-start(f32[256,256]{1,0:T(8,128)} %param.12) | copy-start | bytes 786436
  6.5 33.1 %reduce-scatter.2.cloned.1.call-start = ((), (), s32[]{:S(2)}) async-start(), calls=%async_computation.1 | async-start | bytes 1310720 | tf_op jit(solution)/shard_map/reduce_scatter | solution.py:58
  10.9 64.4 %all-gather.10.cloned.1.call-start = ((), (), s32[]{:S(2)}) async-start(), calls=%async_computation.2 | async-start | bytes 1310720 | tf_op jit(solution)/shard_map/all_gather | solution.py:67
  47.8 32.4 %copy-start.6 = (u32[256]{0:T(256)S(1)}, u32[256]{0:T(256)}, u32[]{:S(2)}) copy-start(u32[256]{0:T(256)} %constant.40) | copy-start | bytes 3076
  47.8 33.0 %copy-start.4 = (s32[512]{0:T(512)S(1)}, s32[512]{0:T(512)}, u32[]{:S(2)}) copy-start(s32[512]{0:T(512)} %param.10) | copy-start | bytes 6148
  47.8 33.0 %copy-start.5 = (bf16[512]{0:T(512)(128)(2,1)S(1)}, bf16[512]{0:T(512)(128)(2,1)}, u32[]{:S(2)}) copy-start(bf16[512]{0:T(512)(128)(2,1)} %param.9) | copy-start | bytes 3076
  49.3 133.2 %all-gather.12.cloned.1.call-start = ((), (), s32[]{:S(2)}) async-start(), calls=%async_computation.3 | async-start | bytes 17039360 | tf_op jit(solution)/shard_map/all_gather | solution.py:11
  75.3 20.5 %copy-start.1 = (f32[1024,256]{1,0:T(8,128)S(1)}, f32[1024,256]{1,0:T(8,128)}, u32[]{:S(2)}) copy-start(f32[1024,256]{1,0:T(8,128)} %all-gather.10.cloned.1.call-done) | copy-start | bytes 3145732
Sparse Core Ops, SparseCore 0:
  11.0 28.5 reduce-scatter.1
  49.4 25.8 all-gather.9
  80.3 102.1 all-gather.11
where the time goes:
time: 325 us; the launch traced here: 322 us
  blocking collectives  193 us (59%)
  waiting for transfers between devices  88.7 us (27%)
  matrix products  22.1 us (7%)
  between operations  14.3 us (4%)
    all_gather x1, blocking collectives, body(): lax.all_gather(rounded, 'tm', axis=0, tiled=True)  128 us
    all_gather x1, blocking collectives, entering(): gathered = jax.tree.map(lambda a: lax.all_gather(a, axis), part)  51.4 us
    all_gather x1, waiting for transfers between devices, entering(): gathered = jax.tree.map(lambda a: lax.all_gather(a, axis), part)  34.4 us
    reduce_scatter x1, waiting for transfers between devices, body(): lax.psum_scatter(local_grams, 'site', scatter_dimension=0, tiled=True)  28.3 us
    all_gather x1, waiting for transfers between devices, body(): lax.all_gather(hour_maps, 'site', axis=0, tiled=True)  26 us
    unnamed x1, blocking collectives  7.69 us
  transfers between devices with their start and end apart: 3, of which 3 were waited for; matrix products, arithmetic and copies ran while one was open for 1% of the time, Pallas kernels for 0%

commit v1 on v0

--- a/solution.py
+++ b/solution.py
@@ -82,7 +82,9 @@
     rounded = jnp.stack(results).astype(jnp.bfloat16)
     return jnp.einsum(
         "hs,ns->hn",
-        lax.all_gather(rounded, "tm", axis=0, tiled=True),
+        jnp.concatenate(
+            lax.all_to_all(jnp.stack([rounded] * lax.axis_size("tm")), "tm", 0, 0), axis=0
+        ),
         site_basis,
         preferred_element_type=jnp.float32,
     ).astype(jnp.bfloat16)

time: 325 us -> 293 us (0.902)
  blocking collectives: 193 us -> 161 us
    all_gather x1 -> x0, blocking collectives: 128 us -> none  [body(): lax.all_gather(rounded, 'tm', axis=0, tiled=True)]
    all_to_all x0 -> x1, blocking collectives: none -> 96.9 us  [body(): lax.all_to_all(jnp.stack([rounded] * lax.axis_size('tm')), 'tm', 0, 0)]
where the time goes in v1:
time: 293 us; the launch traced here: 291 us
  blocking collectives  161 us (55%)
  waiting for transfers between devices  88.7 us (30%)
  matrix products  22 us (8%)
  between operations  14.3 us (5%)
    all_to_all x1, blocking collectives, body(): lax.all_to_all(jnp.stack([rounded] * lax.axis_size('tm')), 'tm', 0, 0)  96.9 us
    all_gather x1, blocking collectives, entering(): gathered = jax.tree.map(lambda a: lax.all_gather(a, axis), part)  51.4 us
    all_gather x1, waiting for transfers between devices, entering(): gathered = jax.tree.map(lambda a: lax.all_gather(a, axis), part)  34.4 us
    reduce_scatter x1, waiting for transfers between devices, body(): lax.psum_scatter(local_grams, 'site', scatter_dimension=0, tiled=True)  28.3 us
    all_gather x1, waiting for transfers between devices, body(): lax.all_gather(hour_maps, 'site', axis=0, tiled=True)  26 us
    unnamed x1, blocking collectives  7.69 us
  transfers between devices with their start and end apart: 3, of which 3 were waited for; matrix products, arithmetic and copies ran while one was open for 1% of the time, Pallas kernels for 0%

profile of v1, /device:TPU:1, one launch (start us, length us, event | category | flops | bytes accessed | tf_op | source)
XLA Modules:
  0.0 290.8 jit_solution(5114779029206567688)
XLA Ops:
  6.5 1.2 copy.8
  7.8 0.7 iota_compare_fusion.3
  8.5 2.4 fusion.4
  10.9 0.4 fusion.68
  11.3 28.3 %reduce-scatter.2.cloned.1.call-done = f32[1,256,256]{2,1,0:T(8,128)} async-done(((f32[4,256,256]{2,1,0:T(8,128)}), f32[1,256,256]{2,1,0:T(8,128)}) %reduce-scatter.2.cloned.1.call-update) | async-done | bytes 262160 | tf_op jit(solution)/shard_map/reduce_scatter | solution.py:58
  39.6 1.1 abs_reduce_fusion
  40.7 0.6 reduce_max.9
  42.0 0.4 convolution_subtract_fusion.7
  42.7 0.4 convolution_subtract_fusion.6
  43.5 0.4 convolution_subtract_fusion.5
  43.9 0.4 fusion.62
  44.3 0.4 convolution_subtract_fusion.4
  45.1 0.4 convolution_subtract_fusion.3
  45.8 0.4 convolution_subtract_fusion.2
  46.6 0.4 convolution_subtract_fusion.1
  47.4 0.4 convolution_subtract_fusion
  48.2 1.1 fusion.69
  49.4 26.0 %all-gather.9.cloned.1.call-done = f32[1024,256]{1,0:T(8,128)} async-done(((f32[256,256]{1,0:T(8,128)}), f32[1024,256]{1,0:T(8,128)}) %all-gather.9.cloned.1.call-update) | async-done | bytes 1048592 | tf_op jit(solution)/shard_map/all_gather | solution.py:67
  75.3 1.5 fusion.21
  76.8 1.3 fusion.32
  78.2 2.0 fusion.38
  80.2 0.6 dynamic-slice
  80.8 1.1 fusion.46
  81.9 7.7 %all-reduce = f32[4,256]{1,0:T(4,128)S(1)} all-reduce(f32[4,256]{1,0:T(4,128)S(1)} %fusion.46), channel_id=7, replica_groups=mesh['tm'=64,'site'=4] {'site'}, use_global_device_ids=true, to_apply=%region_3.4.clone | all-reduce | flops 1024 | bytes 8192
  89.6 0.9 convolution_bitcast_fusion
  90.5 5.3 %all-gather.4 = f32[4,1,256]{2,1,0:T(1,128)S(1)} all-gather(f32[1,1,256]{2,1,0:T(1,128)S(1)} %convolution_bitcast_fusion), channel_id=4, replica_groups=mesh['tm'=64,'site'=4] {'site'}, dimensions={0}, use_global_device_ids=true | all-gather | bytes 5120 | tf_op jit(solution)/shard_map/all_gather | solution.py:68
  96.8 51.4 %all-gather.5 = f32[64,1,256]{2,1,0:T(1,128)S(1)} all-gather(f32[1,1,256]{2,1,0:T(1,128)S(1)} %bitcast.136), channel_id=5, replica_groups=mesh['tm'=64,'site'=4] {'tm'}, dimensions={0}, use_global_device_ids=true | all-gather | bytes 66560 | tf_op jit(solution)/shard_map/all_gather | solution.py:11
  148.1 34.4 %all-gather.11.cloned.1.call-done = f32[16384,256]{1,0:T(8,128)} async-done(((f32[256,256]{1,0:T(8,128)}), f32[16384,256]{1,0:T(8,128)}) %all-gather.11.cloned.1.call-update) | async-done | bytes 16777232 | tf_op jit(solution)/shard_map/all_gather | solution.py:11
  182.5 1.3 while.12
  182.5 1.2 fusion.114
  185.3 96.9 %all_to_all.5 = bf16[64,4,256]{2,1,0:T(4,128)(2,1)S(1)} all-to-all(bf16[64,4,256]{2,1,0:T(4,128)(2,1)S(1)} %stack.17), channel_id=1, replica_groups=mesh['tm'=64,'site'=4] {'tm'}, dimensions={0} | all-to-all | bytes 262144 | tf_op jit(solution)/shard_map/all_to_all | solution.py:86
  282.2 2.1 convolution_convert_fusion
  (53 shorter events, 5.1 us)
Async XLA Ops:
  6.5 275.7 %copy-start = (bf16[4096,256]{1,0:T(8,128)(2,1)S(1)}, bf16[4096,256]{1,0:T(8,128)(2,1)}, u32[]{:S(2)}) copy-start(bf16[4096,256]{1,0:T(8,128)(2,1)} %param.13) | copy-start | bytes 6291460
  6.5 4.4 %copy-start.2 = (f32[256,256]{1,0:T(8,128)S(1)}, f32[256,256]{1,0:T(8,128)}, u32[]{:S(2)}) copy-start(f32[256,256]{1,0:T(8,128)} %param.11) | copy-start | bytes 786436
  6.5 4.4 %copy-start.3 = (f32[256,256]{1,0:T(8,128)S(1)}, f32[256,256]{1,0:T(8,128)}, u32[]{:S(2)}) copy-start(f32[256,256]{1,0:T(8,128)} %param.12) | copy-start | bytes 786436
  6.5 33.1 %reduce-scatter.2.cloned.1.call-start = ((), (), s32[]{:S(2)}) async-start(), calls=%async_computation.2 | async-start | bytes 1310720 | tf_op jit(solution)/shard_map/reduce_scatter | solution.py:58
  10.9 64.4 %all-gather.9.cloned.1.call-start = ((), (), s32[]{:S(2)}) async-start(), calls=%async_computation.3 | async-start | bytes 1310720 | tf_op jit(solution)/shard_map/all_gather | solution.py:67
  47.8 32.4 %copy-start.6 = (u32[256]{0:T(256)S(1)}, u32[256]{0:T(256)}, u32[]{:S(2)}) copy-start(u32[256]{0:T(256)} %constant.40) | copy-start | bytes 3076
  47.8 33.0 %copy-start.4 = (s32[512]{0:T(512)S(1)}, s32[512]{0:T(512)}, u32[]{:S(2)}) copy-start(s32[512]{0:T(512)} %param.10) | copy-start | bytes 6148
  47.8 33.0 %copy-start.5 = (bf16[512]{0:T(512)(128)(2,1)S(1)}, bf16[512]{0:T(512)(128)(2,1)}, u32[]{:S(2)}) copy-start(bf16[512]{0:T(512)(128)(2,1)} %param.9) | copy-start | bytes 3076
  49.3 133.2 %all-gather.11.cloned.1.call-start = ((), (), s32[]{:S(2)}) async-start(), calls=%async_computation.4 | async-start | bytes 17039360 | tf_op jit(solution)/shard_map/all_gather | solution.py:11
  75.3 20.5 %copy-start.1 = (f32[1024,256]{1,0:T(8,128)S(1)}, f32[1024,256]{1,0:T(8,128)}, u32[]{:S(2)}) copy-start(f32[1024,256]{1,0:T(8,128)} %all-gather.9.cloned.1.call-done) | copy-start | bytes 3145732
Sparse Core Ops, SparseCore 0:
  11.0 28.5 reduce-scatter.1
  49.4 25.8 all-gather.8
  80.3 102.1 all-gather.10
